TPU v7x, 32 devices: a whole 2x2x4 slice. The times are simulated.
32 devices in a mesh: grp: 4 (over x, core), wide: 8 (over z, y).
Axes of the slice: x: 2, y: 2, z: 4, core: 2. Of those that a mesh axis runs over, the one named last changes fastest.
Arguments:
- expression: float32 [1024, 4096], P(('grp', 'wide'))
- assignment: int32 [16], replicated, may hold values from 0 to 15, each once
- pairing: int32 [2, 16], replicated, may hold values from 0 to 15, as said below
Outputs:
- cross_scores: float32 [2, 16, 256, 256], P(None, 'wide', 'grp')
Inputs may be any that keep to these rules, and one draw needn't show every extreme that they name: Row r of pairing is round r of one round-robin plan over the 16 panels: every panel has a partner other than itself, and the partner's partner is the panel.
All inputs are finite; a program needn't handle non-finite values.
Results may differ from a plain program's by a relative error of at most 0.0043.
Values may be sent and summed in bfloat16 or wider, within the bound.
No kernel may reach another device: no remote copies, remote signals or barrier semaphores. Data moves between devices by JAX's collectives and lax.ppermute only.
A program may use at most 192 MiB of HBM per device.

v0:
```python
import jax
import jax.numpy as jnp
from jax import lax
from jax.sharding import PartitionSpec as P

PANEL = 256


def cross_terms(received):
    count = received.shape[1]
    cells = received.shape[2]
    width = received.shape[3]
    blocks = received.reshape(count, cells, width // received_panel_width(), received_panel_width())
    own = blocks[:, :, 0]
    partners = blocks[:, :, 1:]
    return jnp.einsum("mca,mcrb->rmab", own, partners, preferred_element_type=jnp.float32)


def received_panel_width():
    return PANEL


def shards(expression, assignment, pairing):
    n_wide = lax.axis_size("wide")
    n_grp = lax.axis_size("grp")
    cells = expression.shape[0]
    pan_dev = assignment.shape[0] // n_wide
    panel = expression.shape[1] // assignment.shape[0]
    rounds = pairing.shape[0]
    total = cells * n_wide * n_grp
    own_ids = assignment.reshape(n_wide, pan_dev, 1)
    partner_ids = pairing[:, assignment].T.reshape(n_wide, pan_dev, rounds)
    panel_ids = jnp.concatenate([own_ids, partner_ids], axis=2)
    columns = (panel_ids[..., None] * panel + jnp.arange(panel, dtype=jnp.int32)).reshape(-1)
    span = (1 + rounds) * panel
    picked = (
        jnp.take(expression, columns, axis=1)
        .reshape(cells, n_wide, pan_dev, span)
        .transpose(1, 2, 0, 3)
    )
    received = lax.all_to_all(picked, "wide", split_axis=0, concat_axis=2, tiled=True)
    sums = lax.psum(
        (
            jnp.sum(received, axis=2, keepdims=True),
            jnp.sum(received * received, axis=2, keepdims=True),
        ),
        "grp",
    )
    mean = sums[0] / total
    var = sums[1] / total - mean * mean
    scaled = ((received - mean) * lax.rsqrt(var + 1e-05)).astype(jnp.bfloat16)
    partial_tiles = cross_terms(scaled)
    rows_dev = panel // n_grp
    summed = lax.psum(partial_tiles, "grp")
    mine = lax.dynamic_slice_in_dim(summed, lax.axis_index("grp") * rows_dev, rows_dev, 2)
    return mine * total ** (-0.5)


def solution(mesh):
    placed = (P(("grp", "wide"), None), P(), P())
    return jax.shard_map(
        shards, mesh=mesh, in_specs=placed, out_specs=P(None, "wide", "grp", None), check_vma=False
    )
```

profile of v0, /device:TPU:0, one launch (start us, length us, event | category | flops | bytes accessed | tf_op | source)
XLA Modules:
  0.0 160.9 jit_solution(13995582573003539010)
XLA Ops:
  6.5 0.0 all-reduce.3.cloned.1.call-start
  6.5 0.7 compare_select_fusion.2
  7.2 0.7 concatenate.11
  7.9 0.1 copy.34
  8.0 0.8 copy.32
  8.8 0.6 gather_fusion
  9.3 0.1 copy.35
  9.4 0.1 copy.36
  9.5 0.1 iota_add_fusion
  9.6 0.1 add.77
  9.7 0.1 reshape.107
  9.8 0.1 compare_select_fusion
  9.9 1.6 %copy.39 = f32[32,4096]{0,1:T(8,128)S(1)} copy(f32[32,4096]{1,0:T(8,128)} %param.3) | data formatting | bytes 1048576 | tf_op args[0]
  11.6 41.0 %gather_fusion.1 = f32[12288,32]{1,0:T(8,128)} fusion(f32[32,4096]{0,1:T(8,128)S(1)} %copy.39, s32[12288]{0:T(1024)S(1)} %broadcast_clamp_fusion), kind=kCustom, calls=%fused_computation.1 | custom fusion | bytes 3194880 | tf_op jit(solution)/shard_map/jit(_take)/gather | solution.py:37
  52.6 4.4 %copy.40 = f32[32,8,2,768]{3,0,2,1:T(8,128)S(1)} copy(f32[32,8,2,768]{0,3,2,1:T(8,128)} %bitcast.26) | data formatting | bytes 3145728 | tf_op jit(solution)/shard_map/jit(_take)/gather | solution.py:37
  56.9 0.2 select_bitcast_fusion
  57.1 44.1 %all_to_all.18 = f32[8,2,32,768]{3,2,1,0:T(8,128)S(1)} all-to-all(f32[8,2,32,768]{3,2,1,0:T(8,128)S(1)} %select_bitcast_fusion), channel_id=1, replica_groups=mesh['grp'=4,'wide'=8] {'wide'}, dimensions={0} | all-to-all | bytes 3145728 | tf_op jit(solution)/shard_map/all_to_all | solution.py:41
  101.2 0.1 copy.41
  101.4 1.9 %all_to_all.16 = f32[2,256,3,256]{3,2,1,0:T(4,128)} reshape(f32[1,2,8,32,768]{4,3,2,1,0:T(8,128)S(1)} %copy.41) | data formatting | bytes 3145728 | tf_op jit(solution)/shard_map/all_to_all | solution.py:41
  103.3 0.2 bitcast_reduce_fusion
  103.4 10.1 %all-reduce = (f32[1,2,1,768]{3,1,2,0:T(2,128)S(1)}, f32[1,2,1,768]{3,1,2,0:T(2,128)S(1)}) all-reduce(f32[1,2,1,768]{3,1,2,0:T(2,128)S(1)} %bitcast.29, f32[1,2,1,768]{3,1,2,0:T(2,128)S(1)} %bitcast.28), channel_id=1, replica_groups=mesh['grp'=4,'wide'=8] {'grp'}, use_global_device_ids=true, to_apply=%region_3.4 | all-reduce | flops 3072 | bytes 24576 | tf_op jit(solution)/shard_map/psum | solution.py:42
  113.6 1.9 %fusion.1 = bf16[2,256,3,256]{3,1,0,2:T(8,128)(2,1)S(1)} fusion(f32[2,256,3,256]{3,2,1,0:T(4,128)} %all_to_all.16, f32[2,3,256]{2,0,1:T(2,128)S(1)} %bitcast.31, f32[2,3,256]{2,0,1:T(2,128)S(1)} %bitcast.30), kind=kLoop, calls=%fused_computation.4 | loop fusion | flops 1179648 | bytes 2371584 | tf_op jit(solution)/shard_map/convert_element_type | solution.py:51
  115.5 1.4 convolution_bitcast_fusion
  116.9 0.0 all-reduce.3.cloned.1.call-update
  116.9 35.5 %all-reduce.3.cloned.1.call-done = f32[2,2,256,256]{3,2,1,0:T(8,128)} async-done(((f32[2,2,256,256]{3,2,1,0:T(8,128)}), f32[2,2,256,256]{3,2,1,0:T(8,128)}) %all-reduce.3.cloned.1.call-update) | async-done | bytes 1048592 | tf_op jit(solution)/shard_map/psum | solution.py:54
  152.4 1.7 %dynamic-slice_multiply_fusion = f32[2,2,64,256]{3,2,1,0:T(8,128)} fusion(f32[2,2,256,256]{3,2,1,0:T(8,128)} %all-reduce.3.cloned.1.call-done, s32[]{:T(128)S(6)} %select_n.32), kind=kLoop, calls=%fused_computation.10 | loop fusion | flops 65536 | bytes 524292 | tf_op jit(solution)/shard_map/mul | solution.py:56
  (6 shorter events, 0.1 us)
Async XLA Ops:
  6.5 145.9 %all-reduce.3.cloned.1.call-start = ((), (), s32[]{:S(2)}) async-start(), calls=%async_computation.1 | async-start | bytes 2097152 | tf_op jit(solution)/shard_map/psum | solution.py:54
Sparse Core Ops, SparseCore 0:
  117.0 35.3 all-reduce.2
where the time goes:
time: 161 us
  blocking collectives  54.2 us (34%)
  local copies, waits for them, and re-layouts  51.5 us (32%)
  waiting for transfers between devices  35.5 us (22%)
  between operations  13.5 us (8%)
  other arithmetic  4.75 us (3%)
    gather x2, local copies, waits for them, and re-layouts, shards(): jnp.take(expression, columns, axis=1).reshape(cells, n_wide, pan_dev, span)  45.4 us
    all_to_all x1, blocking collectives, shards(): lax.all_to_all(picked, 'wide', split_axis=0, concat_axis=2, tiled=True)  44.1 us
    psum x1, waiting for transfers between devices, shards(): summed = lax.psum(partial_tiles, 'grp')  35.5 us
    psum x1, blocking collectives, shards(): lax.psum((jnp.sum(received, axis=2, keepdims=True), jnp.sum(received * re...  10.1 us
  transfers between devices with their start and end apart: 1, of which 1 were waited for; matrix products, arithmetic and copies ran while one was open for 0% of the time, Pallas kernels for 0%

commit v1 on v0

--- a/solution.py
+++ b/solution.py
@@ -4,6 +4,15 @@
 from jax.sharding import PartitionSpec as P
 
 PANEL = 256
+
+
+def doubling_sum(value, axis):
+    n_dev = lax.axis_size(axis)
+    acc, reach = (value, 1)
+    while reach < n_dev:
+        acc = acc + lax.ppermute(acc, axis, [(i, i ^ reach) for i in range(n_dev)])
+        reach = 2 * reach
+    return acc
 
 
 def cross_terms(received):
@@ -51,7 +60,7 @@
     scaled = ((received - mean) * lax.rsqrt(var + 1e-05)).astype(jnp.bfloat16)
     partial_tiles = cross_terms(scaled)
     rows_dev = panel // n_grp
-    summed = lax.psum(partial_tiles, "grp")
+    summed = doubling_sum(partial_tiles, "grp")
     mine = lax.dynamic_slice_in_dim(summed, lax.axis_index("grp") * rows_dev, rows_dev, 2)
     return mine * total ** (-0.5)
 

time: 161 us -> 139 us (0.86)
  between operations: 13.5 us -> 0.14 us
  waiting for transfers between devices: 35.5 us -> 26.3 us
  other arithmetic: 4.75 us -> 1.84 us
  local copies, waits for them, and re-layouts: 51.5 us -> 54.1 us
  starting transfers between devices: 0.01 us -> 1.68 us
    psum x1 -> x0, waiting for transfers between devices: 35.5 us -> none  [shards(): summed = lax.psum(partial_tiles, 'grp')]
    ppermute x0 -> x2, waiting for transfers between devices: none -> 26.3 us  [doubling_sum(): acc = acc + lax.ppermute(acc, axis, [(i, i ^ reach) for i in range(n_dev)])]
    all_to_all x2 -> x3, local copies, waits for them, and re-layouts: 2.04 us -> 3.87 us  [shards(): lax.all_to_all(picked, 'wide', split_axis=0, concat_axis=2, tiled=True)]
    ppermute x0 -> x2, starting transfers between devices: none -> 1.68 us  [doubling_sum(): acc = acc + lax.ppermute(acc, axis, [(i, i ^ reach) for i in range(n_dev)])]
    mul x1, other arithmetic: 1.67 us -> 0.04 us  [shards(): return mine * total ** (-0.5)]
  transfers between devices with their start and end apart: 1 -> 2, of which waited for: 1 -> 2; matrix products, arithmetic and copies ran while one was open for 0% -> 0% of each run, Pallas kernels for 0% -> 0%
where the time goes in v1:
time: 139 us
  blocking collectives  54.2 us (39%)
  local copies, waits for them, and re-layouts  54.1 us (39%)
  waiting for transfers between devices  26.3 us (19%)
  other arithmetic  1.84 us (1%)
  starting transfers between devices  1.68 us (1%)
    gather x2, local copies, waits for them, and re-layouts, shards(): jnp.take(expression, columns, axis=1).reshape(cells, n_wide, pan_dev, span)  45.4 us
    all_to_all x1, blocking collectives, shards(): lax.all_to_all(picked, 'wide', split_axis=0, concat_axis=2, tiled=True)  44.1 us
    ppermute x2, waiting for transfers between devices, doubling_sum(): acc = acc + lax.ppermute(acc, axis, [(i, i ^ reach) for i in range(n_dev)])  26.3 us
    psum x1, blocking collectives, shards(): lax.psum((jnp.sum(received, axis=2, keepdims=True), jnp.sum(received * re...  10.1 us
    all_to_all x3, local copies, waits for them, and re-layouts, shards(): lax.all_to_all(picked, 'wide', split_axis=0, concat_axis=2, tiled=True)  3.87 us
  transfers between devices with their start and end apart: 2, of which 2 were waited for; matrix products, arithmetic and copies ran while one was open for 0% of the time, Pallas kernels for 0%

profile of v1, /device:TPU:0, one launch (start us, length us, event | category | flops | bytes accessed | tf_op | source)
XLA Modules:
  0.0 138.6 jit_solution(7036565224072885322)
XLA Ops:
  0.0 0.7 compare_select_fusion.2
  0.7 0.7 concatenate.11
  1.4 0.1 copy.21
  1.5 0.8 copy.19
  2.2 0.6 gather_fusion
  2.8 0.1 copy.22
  2.9 0.1 copy.23
  3.0 0.1 iota_add_fusion
  3.1 0.1 add.81
  3.2 0.1 reshape.107
  3.3 0.1 compare_select_fusion
  3.4 1.6 %copy.26 = f32[32,4096]{0,1:T(8,128)S(1)} copy(f32[32,4096]{1,0:T(8,128)} %param.3) | data formatting | bytes 1048576 | tf_op args[0]
  5.0 41.0 %gather_fusion.1 = f32[12288,32]{1,0:T(8,128)} fusion(f32[32,4096]{0,1:T(8,128)S(1)} %copy.26, s32[12288]{0:T(1024)S(1)} %broadcast_clamp_fusion), kind=kCustom, calls=%fused_computation.1 | custom fusion | bytes 3194880 | tf_op jit(solution)/shard_map/jit(_take)/gather | solution.py:46
  46.0 4.4 %copy.27 = f32[32,8,2,768]{3,0,2,1:T(8,128)S(1)} copy(f32[32,8,2,768]{0,3,2,1:T(8,128)} %bitcast.27) | data formatting | bytes 3145728 | tf_op jit(solution)/shard_map/jit(_take)/gather | solution.py:46
  50.4 0.2 select_bitcast_fusion
  50.6 44.1 %all_to_all.18 = f32[8,2,32,768]{3,2,1,0:T(8,128)S(1)} all-to-all(f32[8,2,32,768]{3,2,1,0:T(8,128)S(1)} %select_bitcast_fusion), channel_id=1, replica_groups=mesh['grp'=4,'wide'=8] {'wide'}, dimensions={0} | all-to-all | bytes 3145728 | tf_op jit(solution)/shard_map/all_to_all | solution.py:50
  94.7 0.1 copy.28
  94.8 1.9 %all_to_all.16 = f32[2,256,3,256]{3,2,1,0:T(4,128)} reshape(f32[1,2,8,32,768]{4,3,2,1,0:T(8,128)S(1)} %copy.28) | data formatting | bytes 3145728 | tf_op jit(solution)/shard_map/all_to_all | solution.py:50
  96.7 1.8 %copy.29 = f32[2,256,3,256]{1,3,0,2:T(8,128)S(1)} copy(f32[2,256,3,256]{3,2,1,0:T(4,128)} %all_to_all.16) | data formatting | bytes 3145728 | tf_op jit(solution)/shard_map/all_to_all | solution.py:50
  98.5 0.2 bitcast_reduce_fusion
  98.7 10.1 %all-reduce = (f32[1,2,1,768]{3,1,2,0:T(2,128)S(1)}, f32[1,2,1,768]{3,1,2,0:T(2,128)S(1)}) all-reduce(f32[1,2,1,768]{3,1,2,0:T(2,128)S(1)} %bitcast.30, f32[1,2,1,768]{3,1,2,0:T(2,128)S(1)} %bitcast.29), channel_id=1, replica_groups=mesh['grp'=4,'wide'=8] {'grp'}, use_global_device_ids=true, to_apply=%region_3.4 | all-reduce | flops 3072 | bytes 24576 | tf_op jit(solution)/shard_map/psum | solution.py:51
  108.9 0.5 multiply_convert_fusion
  109.4 0.3 convolution_bitcast_fusion
  109.7 0.1 collective-permute-start
  109.8 2.6 %collective-permute-done = f32[2,2,256,256]{3,2,0,1:T(8,128)S(1)} collective-permute-done((f32[2,2,256,256]{3,2,0,1:T(8,128)S(1)}, f32[2,2,256,256]{3,2,0,1:T(8,128)S(1)}, u32[]{:S(2)}, u32[]{:S(2)}) %collective-permute-start) | collective-permute-done | bytes 1048608 | tf_op jit(solution)/shard_map/ppermute | solution.py:13
  112.4 0.1 add.86
  112.6 1.6 %collective-permute-start.1 = (f32[2,2,256,256]{3,2,0,1:T(8,128)S(1)}, f32[2,2,256,256]{3,2,0,1:T(8,128)S(1)}, u32[]{:S(2)}, u32[]{:S(2)}) collective-permute-start(f32[2,2,256,256]{3,2,0,1:T(8,128)S(1)} %add.86), channel_id=1, source_target_pairs={{0,16},{8,24},{16,0},{24,8},{1,17},{9,25},{17,1},{25,9},{2,18},{10... | collective-permute-start | bytes 3145736 | tf_op jit(solution)/shard_map/ppermute | solution.py:13
  114.2 23.7 %collective-permute-done.1 = f32[2,2,256,256]{3,2,0,1:T(8,128)S(1)} collective-permute-done((f32[2,2,256,256]{3,2,0,1:T(8,128)S(1)}, f32[2,2,256,256]{3,2,0,1:T(8,128)S(1)}, u32[]{:S(2)}, u32[]{:S(2)}) %collective-permute-start.1) | collective-permute-done | bytes 1048608 | tf_op jit(solution)/shard_map/ppermute | solution.py:13
  137.9 0.7 copy.31
  (7 shorter events, 0.1 us)
Async XLA Ops:
  109.7 2.7 %collective-permute-start = (f32[2,2,256,256]{3,2,0,1:T(8,128)S(1)}, f32[2,2,256,256]{3,2,0,1:T(8,128)S(1)}, u32[]{:S(2)}, u32[]{:S(2)}) collective-permute-start(f32[2,2,256,256]{3,2,0,1:T(8,128)S(1)} %convolution_bitcast_fusion), channel_id=1, source_target_pairs={{0,8},{8,0},{16,24},{24,16},{1,9},{9,1},{17,25},{25,17},{2,10},{10... | collective-permute-start | bytes 3145736 | tf_op jit(solution)/shard_map/ppermute | solution.py:13
  112.6 25.3 %collective-permute-start.1 = (f32[2,2,256,256]{3,2,0,1:T(8,128)S(1)}, f32[2,2,256,256]{3,2,0,1:T(8,128)S(1)}, u32[]{:S(2)}, u32[]{:S(2)}) collective-permute-start(f32[2,2,256,256]{3,2,0,1:T(8,128)S(1)} %add.86), channel_id=1, source_target_pairs={{0,16},{8,24},{16,0},{24,8},{1,17},{9,25},{17,1},{25,9},{2,18},{10... | collective-permute-start | bytes 3145736 | tf_op jit(solution)/shard_map/ppermute | solution.py:13
